TPU v7x, 32 devices: a whole 2x2x4 slice. The times are simulated.
32 devices in a mesh: dom: 32 (over z, y, x, core).
Axes of the slice: x: 2, y: 2, z: 4, core: 2. Of those that a mesh axis runs over, the one named last changes fastest.
Arguments:
- start_state: float32 [504, 8192], P(None, 'dom'), may hold values from -6 to 6
- material: float32 [3, 8192], P(None, 'dom'), may hold values from 0.35 to 1.4
- geometry: float32 [3, 8192], P(None, 'dom'), may hold values from 0.6 to 1.6
- clusters: int32 [8192], P('dom'), may hold values from 0 to 1, as said below
- neighbours: int32 [4, 8192], P(None, 'dom'), may hold values from -1 to 8191, as said below
- orientation: int32 [4, 8192], P(None, 'dom'), may hold values from 0 to 11
- stiffness: float32 [3, 56, 56], replicated, may hold values from -0.75 to 0.75
- face_trace: float32 [4, 21, 56], replicated, may hold values from -0.75 to 0.75
- face_lift: float32 [4, 56, 21], replicated, may hold values from -1.25 to 1.25
- face_turns: float32 [3, 21, 21], replicated, may hold values from -1.25 to 1.25
- cotangent: float32 [504, 8192], P(None, 'dom'), may hold values from -0.27 to 0.27
Outputs:
- final_state: float32 [504, 8192], P(None, 'dom')
- material_grad: float32 [3, 8192], P(None, 'dom')
Inputs may be any that keep to these rules, and one draw needn't show every extreme that they name: `clusters`: 1 marks a fine element; a device's block of 256 elements holds at most 128 fine ones, and some block holds exactly 128. `neighbours`: element n sits on device n // 256. A neighbour on another device is 1 to 4 devices away counted around the device cycle, or exactly half the cycle away. For every device and every such distance (up or down), at most 16 of the device's faces name elements there; on every device exactly 16 faces name elements half the cycle away.
All inputs are finite; a program needn't handle non-finite values.
Results may differ from a plain program's by a relative error of at most 0.0001.
Values sent between devices are 32-bit elements; how exact they have to be, the bound alone decides.
A program may use at most 192 MiB of HBM per device.

v0:
```python
import functools

import jax
import jax.numpy as jnp
from jax import lax
from jax.experimental import pallas as pl
from jax.experimental.pallas import tpu as pltpu
from jax.sharding import PartitionSpec as P

VARS = 9
TERMS = 6
REACH = 4
CAP = 16
FINE_DEV = 128
LANES = 2 * REACH + 1
SLOTS = LANES * CAP
STEPS = TERMS - 1
f32, bf16, i32 = jnp.float32, jnp.bfloat16, jnp.int32

dt_step = 0.5
root_third = 0.5773502691896258
H = 0.5 * dt_step

A0 = H
STEP_SCALE = [H * H / 2.0] + [H / (k + 2.0) for k in range(1, STEPS)]
C_OVER_A = [2.0 ** (k + 1) - 1.0 for k in range(TERMS)]

NEED = [(0, 1), (1, 1), (2, 1), (0, 2), (1, 2), (2, 2), (0, 3), (0, 3), (0, 3)]
PAIRS = [((6, 7), 0, 3), ((8, 3), 0, 3), ((0, 1), 0, 2), ((4, 2), 1, 2), ((5,), 2, 2)]
READS = [
    {3: 7, 5: 8, 6: 0, 7: 3, 8: 5},
    {3: 6, 4: 8, 6: 3, 7: 1, 8: 4},
    {4: 7, 5: 6, 6: 5, 7: 4, 8: 2},
]


def up_to(n, m):
    return -(-n // m) * m


def halves(x):
    high = x.astype(bf16)
    return high, (x - high.astype(f32)).astype(bf16)


def padded(x, rows):
    if x.shape[0] == rows:
        return x
    return jnp.concatenate([x, jnp.zeros((rows - x.shape[0], x.shape[1]), f32)], axis=0)


def right3(x, rows):
    high, low = halves(padded(x, rows))
    return jnp.concatenate([high, high, low], axis=0)


def left3(a):
    high = a.astype(bf16).astype(f32)
    return jnp.concatenate([high, a - high, high], axis=1).astype(bf16)


def stack2(x, rows):
    return jnp.concatenate(halves(padded(x, rows)), axis=0)


def mm(a, b):
    return jnp.dot(a, b, preferred_element_type=f32)


def mm_t(a, b):
    return lax.dot_general(a, b, (((1,), (1,)), ((), ())), preferred_element_type=f32)


def add(*terms):
    total = None
    for t in terms:
        if t is not None:
            total = t if total is None else total + t
    return total


def blocks(ref, size, base=0):
    return [ref[base + v * size : base + (v + 1) * size, :] for v in range(VARS)]


def put(ref, values, base=0):
    size = values[0].shape[0]
    for v in range(VARS):
        ref[base + v * size : base + (v + 1) * size, :] = values[v]


def row(ref, n):
    return ref[n : n + 1, :]


class Mat:
    def __init__(self, con, base, geo):
        self.lam, self.mu2 = row(con, base), row(con, base + 1)
        self.mg = [row(con, base + 2 + a) for a in range(3)]
        self.rg = [row(con, base + 5 + a) for a in range(3)]
        self.g = [row(geo, a) for a in range(3)]


def forward_mix(p, m):
    t = [m.g[a] * p(6 + a, a) for a in range(3)]
    spread = m.lam * (t[0] + t[1] + t[2])
    return [
        spread + m.mu2 * t[0],
        spread + m.mu2 * t[1],
        spread + m.mu2 * t[2],
        m.mg[0] * p(7, 0) + m.mg[1] * p(6, 1),
        m.mg[1] * p(8, 1) + m.mg[2] * p(7, 2),
        m.mg[0] * p(8, 0) + m.mg[2] * p(6, 2),
        m.rg[0] * p(0, 0) + m.rg[1] * p(3, 1) + m.rg[2] * p(5, 2),
        m.rg[0] * p(3, 0) + m.rg[1] * p(1, 1) + m.rg[2] * p(4, 2),
        m.rg[0] * p(5, 0) + m.rg[1] * p(4, 1) + m.rg[2] * p(2, 2),
    ]


def normal_mix(r, m):
    u = m.lam * (r[0] + r[1] + r[2])
    return [u + m.mu2 * r[a] for a in range(3)] + list(r[3:])


def backward_mix(p, m):
    return [
        m.rg[0] * p(6, 0),
        m.rg[1] * p(7, 1),
        m.rg[2] * p(8, 2),
        m.rg[0] * p(7, 0) + m.rg[1] * p(6, 1),
        m.rg[1] * p(8, 1) + m.rg[2] * p(7, 2),
        m.rg[0] * p(8, 0) + m.rg[2] * p(6, 2),
        m.g[0] * p(0, 0) + m.mg[1] * p(3, 1) + m.mg[2] * p(5, 2),
        m.g[1] * p(1, 1) + m.mg[0] * p(3, 0) + m.mg[2] * p(4, 2),
        m.g[2] * p(2, 2) + m.mg[1] * p(4, 1) + m.mg[0] * p(5, 0),
    ]


def products(mat, values):
    size, width = values[0].shape
    pitch = mat.shape[0] // 4
    out = {}
    if width == FINE_DEV:
        groups = PAIRS
    else:
        groups = [((v,), s, c) for v, (s, c) in enumerate(NEED)]
    for names, start, count in groups:
        x = [values[v] for v in names]
        x = x[0] if len(x) == 1 else jnp.concatenate(x, axis=1)
        y = mm(mat[start * pitch : (start + count) * pitch, :], right3(x, pitch))
        for n, v in enumerate(names):
            for i in range(count):
                out[v, (start + i) % 3] = y[
                    i * pitch : i * pitch + size, n * width : (n + 1) * width
                ]
    return lambda v, axis: out[v, axis]


def apply_step(mat, values, m):
    return forward_mix(products(mat, values), m)


def apply_back(mat, values, m):
    return backward_mix(products(mat, normal_mix(values, m)), m)


def fold8(x):
    total = x[0:8]
    for n in range(8, x.shape[0], 8):
        total = total + x[n : n + 8]
    return total


def group_sums(r, x):
    mixed = (r[0] + r[1] + r[2]) * (x[0] + x[1] + x[2])
    groups = [add(*[r[v] * x[v] for v in range(g, g + 3)]) for g in (0, 3, 6)]
    return [fold8(g) for g in [mixed] + groups]


def plus(total, more):
    return more if total is None else [a + b for a, b in zip(total, more)]


def narrow(x, hot_c, rows):
    y = mm_t(stack2(x, rows), hot_c)
    return y[: x.shape[0]] + y[rows : rows + x.shape[0]]


def widen(x, hot_c2, rows):
    high, low = halves(padded(x, rows))
    return mm(jnp.concatenate([high, low], axis=1), hot_c2)[: x.shape[0]]


def trace_faces(tr, window, own, own_hl, fb, elems):
    size = window.shape[0] // VARS
    rows = own_hl.shape[0] // 2
    for v in range(VARS):
        t = mm(tr[...], right3(window[v * size : (v + 1) * size, :], tr.shape[1] // 3))
        for g in range(4):
            own[v * fb : (v + 1) * fb, g * elems : (g + 1) * elems] = t[g * fb : (g + 1) * fb]
    for g in range(4):
        cols = slice(g * elems, (g + 1) * elems)
        high, low = halves(padded(own[:, cols], rows))
        own_hl[:rows, cols] = high
        own_hl[rows:, cols] = low


def turn_blocks(mat, x, which):
    fb = x[0].shape[0]
    first, second = which == 0, which == 1
    out = []
    for n in range(0, len(x), 2):
        pair = x[n] if n + 1 == len(x) else jnp.concatenate(x[n : n + 2], axis=0)
        y = mm(mat[...], right3(pair, 2 * fb))
        for i in range(min(2, len(x) - n)):
            part = [y[o * 2 * fb + i * fb : o * 2 * fb + (i + 1) * fb] for o in range(3)]
            out.append(jnp.where(first, part[0], jnp.where(second, part[1], part[2])))
    return out


def split_rows(x, fb):
    return [x[v * fb : (v + 1) * fb] for v in range(VARS)]


def local_outer(own_hl, hot, turn, tn, out, fb, elems, f):
    rows = own_hl.shape[0] // 2
    cols = slice(f * elems, (f + 1) * elems)
    y = mm(own_hl[...], hot[:, cols])
    raw = y[: VARS * fb] + y[rows : rows + VARS * fb]
    turned = turn_blocks(tn, split_rows(raw, fb), turn[f : f + 1, :])
    out[:, cols] = jnp.concatenate(turned, axis=0)


def serve(hot_in, own_hl, tx):
    rows = own_hl.shape[0] // 2
    tx[:, :rows] = mm_t(hot_in[...], own_hl[:rows, :]) + mm_t(hot_in[...], own_hl[rows:, :])
    tx[:, rows:] = jnp.zeros((tx.shape[0], tx.shape[1] - rows), f32)


def flipped(rx):
    x = rx[...]
    return padded(x, up_to(x.shape[0], 128)).T[:, : x.shape[0]]


def face_rows(f, x, fc):
    if f == 3:
        return forward_mix(lambda v, axis: x[v], fc)
    axis = 2 - f
    kl, kp, _, km, kr = fc
    t = x[6 + axis]
    rows = [kl * t] * 3 + [None] * 6
    rows[axis] = kp * t
    for v, source in READS[axis].items():
        rows[v] = (km if v < 6 else kr) * x[source]
    return rows


def face_rows_back(f, r, fc):
    if f == 3:
        s = normal_mix(r, fc)
        return backward_mix(lambda v, axis: s[v], fc)
    axis = 2 - f
    kl, _, k2, km, kr = fc
    out = [None] * VARS
    out[6 + axis] = kl * (r[0] + r[1] + r[2]) + k2 * r[axis]
    for v, source in READS[axis].items():
        out[source] = (km if v < 6 else kr) * r[v]
    return out


def face_consts(f, fcon, con):
    if f == 3:
        m = Mat.__new__(Mat)
        m.lam, m.mu2 = row(fcon, 15), row(fcon, 16)
        m.mg = [row(fcon, 17 + a) for a in range(3)]
        m.rg = [row(fcon, 20 + a) for a in range(3)]
        m.g = [row(fcon, 23 + a) for a in range(3)]
        return m
    return [row(fcon, 5 * f + n) for n in range(5)]


def far_side(rx, slot_turn, tn, hot_slot, out_loc, fb):
    rows = up_to(VARS * fb, 16)
    turned = turn_blocks(tn, split_rows(flipped(rx), fb), slot_turn[0:1, :])
    high_low = stack2(jnp.concatenate(turned, axis=0), rows)

    def far(f, elems):
        cols = slice(f * elems, (f + 1) * elems)
        y = mm(high_low, hot_slot[:, cols])
        return out_loc[:, cols] + (y[: VARS * fb] + y[rows : rows + VARS * fb])

    return far


def surface(lf, own, far, fcon, con, fb, elems, jump_ref, flux_ref):
    half_speed = row(fcon, 26)
    fluxes = [[] for _ in range(VARS)]
    for f in range(4):
        cols = slice(f * elems, (f + 1) * elems)
        a, b = split_rows(own[:, cols], fb), split_rows(far(f, elems), fb)
        rows = face_rows(f, [x + y for x, y in zip(a, b)], face_consts(f, fcon, con))
        for v in range(VARS):
            jump = a[v] - b[v]
            flux = add(half_speed * jump, rows[v])
            jump_ref[v * fb : (v + 1) * fb, cols] = jump
            flux_ref[v * fb : (v + 1) * fb, cols] = flux
            fluxes[v].append(flux)
    return [mm(lf[...], right3(jnp.concatenate(x, axis=0), 4 * fb)) for x in fluxes]


def face_sums(lifted, jump_ref, flux_ref, half_speed, fb, elems):
    total, speed = None, None
    for f in range(4):
        cols = slice(f * elems, (f + 1) * elems)
        r, d, x = [split_rows(ref[:, cols], fb) for ref in (lifted, jump_ref, flux_ref)]
        of_jump, of_flux = group_sums(r, d), group_sums(r, x)
        total = plus(total, [a - half_speed * b for a, b in zip(of_flux, of_jump)])
        more = of_jump[1] + of_jump[2] + of_jump[3]
        speed = more if speed is None else speed + more
    return total, speed


def faces_cot(seed, lt, tnt, turn, extra, fcon, con, lifted, own_cot, x_hl, fb, elems):
    half_speed = row(fcon, 26)
    rows = x_hl.shape[0] // 2
    for v in range(VARS):
        y = mm(lt[...], right3(seed[v], lt.shape[1] // 3))
        for f in range(4):
            lifted[v * fb : (v + 1) * fb, f * elems : (f + 1) * elems] = y[f * fb : (f + 1) * fb]
    for f in range(4):
        cols = slice(f * elems, (f + 1) * elems)
        r = split_rows(lifted[:, cols], fb)
        back = face_rows_back(f, r, face_consts(f, fcon, con))
        x = []
        for v in range(VARS):
            side = half_speed * r[v]
            own_cot[v * fb : (v + 1) * fb, cols] = add(side, back[v])
            x.append(-side if back[v] is None else back[v] - side)
        turned = turn_blocks(tnt, x, turn[f : f + 1, :])
        if extra is not None:
            turned.append(extra[:, cols])
        high, low = halves(padded(jnp.concatenate(turned, axis=0), rows))
        x_hl[:rows, cols] = high
        x_hl[rows:, cols] = low


def send_cot(hot_slot, x_hl, tx):
    serve(hot_slot, x_hl, tx)


def scatter_local(own_cot, x_hl, hot, fb, elems, g):
    rows = x_hl.shape[0] // 2
    cols = slice(g * elems, (g + 1) * elems)
    y = mm_t(x_hl[...], hot[cols, :])
    own_cot[:, cols] = own_cot[:, cols] + (y[: VARS * fb] + y[rows : rows + VARS * fb])


def faces_back(own_cot, rx, hot_in, trt, fb, elems):
    rows = up_to(VARS * fb, 16)
    arrived = stack2(flipped(rx)[: VARS * fb], rows)
    for g in range(4):
        cols = slice(g * elems, (g + 1) * elems)
        y = mm(arrived, hot_in[:, cols])
        own_cot[:, cols] = own_cot[:, cols] + (y[: VARS * fb] + y[rows : rows + VARS * fb])
    out = []
    for v in range(VARS):
        x = [own_cot[v * fb : (v + 1) * fb, g * elems : (g + 1) * elems] for g in range(4)]
        out.append(mm(trt[...], right3(jnp.concatenate(x, axis=0), 4 * fb)))
    return out


def weave(steps, pieces):
    done = 0
    for n, step in enumerate(steps):
        step()
        until = (n + 1) * len(pieces) // len(steps)
        for piece in pieces[done:until]:
            piece()
        done = until


def peers_of(devices):
    me = lax.axis_index("dom")
    shifts = [n + 1 for n in range(REACH)] + [-(n + 1) for n in range(REACH)] + [devices // 2]
    return [
        [lax.rem(me + sign * s + 2 * devices, devices) for s in shifts] for sign in (1, -1)
    ]


def send_all(peers, src, dst, send_sems, recv_sems, base=0):
    copies = []
    for n in reversed(range(LANES)):
        rows = pl.ds(n * CAP, CAP)
        copy = pltpu.make_async_remote_copy(
            src_ref=src.at[rows],
            dst_ref=dst.at[rows],
            send_sem=send_sems.at[base + n],
            recv_sem=recv_sems.at[base + n],
            device_id=(peers[n],),
            device_id_type=pl.DeviceIdType.MESH,
        )
        copy.start()
        copies.append(copy)
    return copies


def one_hot(mask):
    return jnp.where(mask, 1.0, 0.0).astype(bf16)


def face_places(
    devices, neighbours, orientation, fine, hot, hot_slot, hot_c, turn, slot_turn, extra
):
    elems = neighbours.shape[1]
    me = lax.axis_index("dom")
    at = lax.broadcasted_iota(i32, (16, elems), 0)
    square = (elems, elems)
    at_n, at_e = lax.broadcasted_iota(i32, square, 0), lax.broadcasted_iota(i32, square, 1)
    at_s = lax.broadcasted_iota(i32, (SLOTS, elems), 0)
    at_8 = lax.broadcasted_iota(i32, (8, elems), 0)
    earlier = one_hot(at_n <= at_e)
    lanes, marks, keys = [], [], []
    for f in range(4):
        cols = slice(f * elems, (f + 1) * elems)
        name, code = neighbours[f : f + 1, :], orientation[f : f + 1, :]
        far_face = sum(jnp.where(code >= 3 * g, 1, 0) for g in (1, 2, 3))
        turn[f : f + 1, :] = code - 3 * far_face
        present = name >= 0
        safe = jnp.maximum(name, 0)
        owner = jnp.floor((safe.astype(f32) + 0.5) * (1.0 / elems)).astype(i32)
        index = safe - owner * elems
        away = owner - me
        away = jnp.where(away < 0, away + devices, away)
        keys.append((cols, present & (away == 0), far_face, index))
        lane = jnp.where(
            away <= REACH,
            away - 1,
            jnp.where(away >= devices - REACH, REACH + devices - away - 1, 2 * REACH),
        )
        lane = jnp.where(present & (away != 0), lane, LANES)
        lanes.append(lane)
        marks.append(jnp.where(at == lane, 1.0, 0.0))
        index_f, face_f = index.astype(f32), far_face.astype(f32)
        extra[:, cols] = jnp.where(
            at_8 == 0, index_f, jnp.where(at_8 == 1, face_f, jnp.where(at_8 == 2, 1.0, 0.0))
        )
    is_fine = fine[...] == 1
    marks.append(jnp.where((at == 0) & is_fine, 1.0, 0.0))
    run = mm(jnp.concatenate(marks, axis=0).astype(bf16), earlier)
    carry = jnp.zeros((16, 1), f32)
    for f in range(4):
        cols = slice(f * elems, (f + 1) * elems)
        mine = run[16 * f : 16 * f + 16]
        rank = jnp.sum((mine + carry - 1.0) * marks[f], axis=0, keepdims=True).astype(i32)
        carry = carry + mine[:, elems - 1 :]
        slot = jnp.where(lanes[f] < LANES, lanes[f] * CAP + rank, -1)
        hot_slot[:, cols] = one_hot(at_s == slot)
    rank = jnp.where(is_fine, run[64:65].astype(i32) - 1, -1)
    picked = one_hot(lax.broadcasted_iota(i32, (FINE_DEV, elems), 0) == rank)
    hot_c[:FINE_DEV, :] = picked
    hot_c[FINE_DEV:, :] = picked
    turns = jnp.concatenate([turn[f : f + 1, :].astype(f32) for f in range(4)], axis=1)
    turns = jnp.broadcast_to(turns, (16, 4 * elems)).astype(bf16)
    slot_turn[...] = mm_t(turns, hot_slot[...])

    def fill(cols, local, far_face, index):
        names = at_n.astype(f32).astype(bf16)
        for g in range(4):
            key = jnp.where(local & (far_face == g), index, -1).astype(f32).astype(bf16)
            hot[g * elems : (g + 1) * elems, cols] = jnp.where(
                names == key, jnp.ones(square, bf16), jnp.zeros(square, bf16)
            )

    return [functools.partial(fill, *key) for key in keys]


def constants(mat_ref, geo_ref, con, fcon):
    lam, mu, rinv = [row(mat_ref, n) for n in range(3)]
    geo = [row(geo_ref, n) for n in range(3)]
    rows = [lam, 2.0 * mu] + [mu * g for g in geo] + [rinv * g for g in geo]
    base = jnp.concatenate(rows, axis=0)
    for n, scale in enumerate([-1.0] + STEP_SCALE):
        con[8 * n : 8 * n + 8, :] = scale * base
    rows = []
    for f in range(3):
        h = 0.5 * geo[2 - f]
        rows += [lam * h, (lam + 2.0 * mu) * h, 2.0 * mu * h, mu * h, rinv * h]
    h = [(-0.5 * root_third) * g for g in geo]
    rows += [lam, 2.0 * mu] + [mu * x for x in h] + [rinv * x for x in h] + h
    rows += [0.5 * jnp.sqrt((lam + 2.0 * mu) * rinv)]
    for n, x in enumerate(rows):
        fcon[n : n + 1, :] = x


def pitched(pad, matrices):
    pad[...] = jnp.zeros(pad.shape, f32)
    for n, x in enumerate(matrices):
        pad[n, : x.shape[0], : x.shape[1]] = x
    return [pad[n] for n in range(len(matrices))]


def turn_matrix(pad, matrices):
    zero = jnp.zeros(pad.shape[1:], f32)
    out = []
    for x in pitched(pad, matrices):
        out += [jnp.concatenate([x, zero], axis=1), jnp.concatenate([zero, x], axis=1)]
    return left3(jnp.concatenate(out, axis=0))


def step_kernel(
    devices,
    state_in, cot_in, mat_in, geo_in, fine_in, neighbours_in, orientation_in, stiffness_in,
    trace_in, lift_in, turns_in,
    final, grad,
    state, cot, mat_ref, geo_ref, stiffness, face_trace, face_lift, face_turns,
    w1, wc, w2, coarse, seed1, middle, vol1, vol2, cur, direct2,
    q1, q2, hist,
    own, lifted1, lifted2, out_loc, own_cot1, own_cot2, jump, flux,
    tx0, tx1, tx2, tx3, rx0, rx1, rx2, rx3,
    con, fcon, con_f, geo_f, extra, slot_turn,
    k_pad, t_pad, l_pad, n_pad,
    ks, kt, tr, lt, trt, lf, tn, tnt, hot, hot_slot, hot_in, hot_c, own_hl, x_hl1, x_hl2,
    fine, neighbours, orientation, turn, load_sems, send_sems, recv_sems,
):
    loads = [
        pltpu.make_async_copy(src, dst, load_sems.at[n])
        for n, (src, dst) in enumerate([
            (neighbours_in, neighbours), (orientation_in, orientation), (mat_in, mat_ref),
            (geo_in, geo_ref), (fine_in, fine), (stiffness_in, stiffness),
            (trace_in, face_trace), (lift_in, face_lift), (turns_in, face_turns),
            (cot_in, cot), (state_in, state),
        ])
    ]
    for load in loads:
        load.start()
    up, down = peers_of(devices)
    barrier = pltpu.get_barrier_semaphore()
    for peer in up:
        pl.semaphore_signal(
            barrier, inc=1, device_id=(peer,), device_id_type=pl.DeviceIdType.MESH
        )
    elems = state.shape[1]
    count = state.shape[0]
    size = count // VARS
    fb = t_pad.shape[1]
    wide = up_to(count, 16)
    part = functools.partial

    for load in loads[:9]:
        load.wait()
    constants(mat_ref, geo_ref, con, fcon)
    trace = jnp.concatenate(pitched(t_pad, [face_trace[:, g, :] for g in range(4)]), axis=0)
    tr[...] = left3(trace)
    trt[...] = left3(trace.T)[:size]
    lift = jnp.concatenate(pitched(l_pad, [-face_lift[:, f, :] for f in range(4)]), axis=0)
    lt[...] = left3(lift)
    lf[...] = left3(lift.T)[:size]
    turns = [face_turns[o] for o in range(3)]
    tn[...] = turn_matrix(n_pad, turns)
    tnt[...] = turn_matrix(n_pad, [x.T for x in turns])
    hot_fills = face_places(
        devices, neighbours, orientation, fine, hot, hot_slot, hot_c, turn, slot_turn, extra
    )
    base, half_speed = Mat(con, 0, geo_ref), row(fcon, 26)

    loads[9].wait()
    seed2 = blocks(cot, size)
    faces_cot(seed2, lt, tnt, turn, extra, fcon, con, lifted2, own_cot2, x_hl2, fb, elems)
    serve(hot_slot, x_hl2, tx0)
    pl.semaphore_wait(barrier, LANES)
    sent0 = send_all(up, tx0, rx0, send_sems, recv_sems, 0)

    stiff = pitched(k_pad, [stiffness[d] for d in range(3)])
    ks[...] = left3(jnp.concatenate(stiff + stiff[:1], axis=0))
    stiff = [x.T for x in stiff]
    kt[...] = left3(jnp.concatenate(stiff + stiff[:1], axis=0))
    is_fine = fine[...] == 1
    loads[10].wait()

    def step1(k):
        old = blocks(state, size) if k == 0 else blocks(q1, size, (k - 1) * count)
        put(q1, apply_step(ks, old, Mat(con, 8 * (k + 1), geo_ref)), k * count)

    def scatter(own_cot, x_hl):
        return [part(scatter_local, own_cot, x_hl, hot, fb, elems, g) for g in range(4)]

    def gather():
        return [
            part(local_outer, own_hl, hot, turn, tn, out_loc, fb, elems, f) for f in range(4)
        ]

    weave([part(step1, k) for k in range(STEPS)], hot_fills + scatter(own_cot2, x_hl2))
    for v in range(VARS):
        rows = slice(v * size, (v + 1) * size)
        terms = [A0 * state[rows, :]]
        terms += [q1[k * count + v * size : k * count + (v + 1) * size, :] for k in range(STEPS)]
        w1[rows, :] = add(*terms)
        later = add(*[c * t if c != 1.0 else t for c, t in zip(C_OVER_A, terms)])
        wc[rows, :] = jnp.where(is_fine, 0.0, later)
    trace_faces(tr, w1, own, own_hl, fb, elems)
    put(direct2, apply_back(ks, seed2, base))
    for copy in sent0:
        copy.wait()

    key = rx0[:, VARS * fb : VARS * fb + 3]
    key = jnp.where(key[:, 2:3] > 0.5, key[:, 1:2] * float(elems) + key[:, 0:1], -1.0)
    at = lax.broadcasted_iota(i32, (SLOTS, 4 * elems), 1)
    hot_in[...] = one_hot(at == key.astype(i32))
    serve(hot_in, own_hl, tx1)
    sent1 = send_all(down, tx1, rx1, send_sems, recv_sems, LANES)

    back = faces_back(own_cot2, rx0, hot_in, trt, fb, elems)
    back = [a + b for a, b in zip(back, blocks(direct2, size))]
    put(coarse, [jnp.where(is_fine, 0.0, x) for x in back])
    seeds = split_rows(narrow(jnp.concatenate(back, axis=0), hot_c[:FINE_DEV, :], wide), size)
    put(hist, seeds, (STEPS - 1) * count)
    narrow_con = mm_t(
        jnp.concatenate(
            halves(con[0:16, :]) + halves(padded(geo_ref[...], 16)), axis=0
        ),
        hot_c[:FINE_DEV, :],
    )
    geo_f[...] = narrow_con[32:40] + narrow_con[48:56]
    for n, scale in enumerate(STEP_SCALE):
        con_f[8 * n : 8 * n + 8, :] = -scale * (narrow_con[0:8] + narrow_con[16:24])

    def back2(k):
        r = apply_back(kt, blocks(hist, size, k * count), Mat(con_f, 8 * k, geo_f))
        scale = A0 if k == 0 else 1.0
        direct = blocks(hist, size, (STEPS - 1) * count)
        r = [a + (b if k else scale * b) for a, b in zip(r, direct)]
        if k:
            put(hist, r, (k - 1) * count)
        else:
            seed1[...] = widen(jnp.concatenate(r, axis=0), hot_c[...], wide) + cot[...]

    def volume(out, window):
        put(out, apply_step(kt, blocks(window, size), base))

    weave([part(back2, k) for k in range(STEPS - 1, -1, -1)], gather() + [part(volume, vol1, w1)])
    faces_cot(
        blocks(seed1, size), lt, tnt, turn, None, fcon, con, lifted1, own_cot1, x_hl1, fb, elems
    )
    serve(hot_slot, x_hl1, tx3)
    sent3 = send_all(up, tx3, rx3, send_sems, recv_sems, 2 * LANES)
    for copy in sent1:
        copy.wait()

    far = far_side(rx1, slot_turn, tn, hot_slot, out_loc, fb)
    change = surface(lf, own, far, fcon, con, fb, elems, jump, flux)
    put(middle, [
        s + m + c for s, m, c in zip(blocks(state, size), blocks(vol1, size), change)
    ])
    start = split_rows(narrow(middle[...], hot_c[:FINE_DEV, :], wide), size)
    first = [A0 * x for x in start]

    def step2(k):
        old = start if k == 0 else blocks(q2, size, (k - 1) * count)
        put(q2, apply_step(ks, old, Mat(con_f, 8 * k, geo_f)), k * count)

    def direct1():
        put(cur, apply_back(ks, blocks(seed1, size), base))

    weave(
        [part(step2, k) for k in range(STEPS)], scatter(own_cot1, x_hl1) + [direct1]
    )
    window = [
        add(first[v], *[
            q2[k * count + v * size : k * count + (v + 1) * size, :] for k in range(STEPS)
        ])
        for v in range(VARS)
    ]
    w2[...] = widen(jnp.concatenate(window, axis=0), hot_c[...], wide) + wc[...]
    sums, speed = face_sums(lifted1, jump, flux, half_speed, fb, elems)
    trace_faces(tr, w2, own, own_hl, fb, elems)
    serve(hot_in, own_hl, tx2)
    sent2 = send_all(down, tx2, rx2, send_sems, recv_sems, 3 * LANES)

    sums = plus(sums, group_sums(blocks(seed1, size), blocks(vol1, size)))
    fine_sums = None
    for k in range(STEPS):
        fine_sums = plus(
            fine_sums, group_sums(blocks(hist, size, k * count), blocks(q2, size, k * count))
        )
    fine_sums = [jnp.sum(x, axis=0, keepdims=True) for x in fine_sums]
    fine_sums = widen(jnp.concatenate(fine_sums + fine_sums, axis=0), hot_c[...], 16)
    for copy in sent3:
        copy.wait()
    back = faces_back(own_cot1, rx3, hot_in, trt, fb, elems)
    put(seed1, [a + b for a, b in zip(back, blocks(cur, size))])
    chain = [sums]

    def back1(k):
        r = [a + C_OVER_A[k] * b for a, b in zip(blocks(seed1, size), blocks(coarse, size))]
        if k < STEPS:
            old = blocks(cur, size)
            r = [a + b for a, b in zip(r, apply_back(kt, old, Mat(con, 8 * (k + 1), geo_ref)))]
        put(cur, r)
        chain[0] = plus(
            chain[0], group_sums(blocks(cur, size), blocks(q1, size, (k - 1) * count))
        )

    weave([part(back1, k) for k in range(STEPS, 0, -1)], gather() + [part(volume, vol2, w2)])
    sums = plus(chain[0], group_sums(seed2, blocks(vol2, size)))
    for copy in sent2:
        copy.wait()

    far = far_side(rx2, slot_turn, tn, hot_slot, out_loc, fb)
    change = surface(lf, own, far, fcon, con, fb, elems, jump, flux)
    put(final, [
        s + m + c for s, m, c in zip(blocks(middle, size), blocks(vol2, size), change)
    ])
    more, more_speed = face_sums(lifted2, jump, flux, half_speed, fb, elems)
    sums = [jnp.sum(a + b, axis=0, keepdims=True) for a, b in zip(sums, more)]
    sums = [a + fine_sums[n : n + 1] for n, a in enumerate(sums)]
    g_speed = 0.5 * jnp.sum(speed + more_speed, axis=0, keepdims=True)
    lam, mu, rinv = [row(mat_ref, n) for n in range(3)]
    wave = jnp.sqrt((lam + 2.0 * mu) * rinv)
    g_lam = sums[0] / (3.0 * lam + 2.0 * mu)
    g_mu = (sums[1] - lam * g_lam + sums[2]) / mu
    g_speed = g_speed / wave
    grad[...] = jnp.concatenate(
        [
            g_lam + 0.5 * g_speed * rinv,
            g_mu + g_speed * rinv,
            sums[3] / rinv + 0.5 * g_speed * (lam + 2.0 * mu),
        ],
        axis=0,
    )


def finish_kernel(final, grad, final_out, grad_out, sems):
    copies = [
        pltpu.make_async_copy(final, final_out, sems.at[0]),
        pltpu.make_async_copy(grad, grad_out, sems.at[1]),
    ]
    for copy in copies:
        copy.start()
    for copy in copies:
        copy.wait()


def body(
    start_state, material, geometry, clusters, neighbours, orientation,
    stiffness, face_trace, face_lift, face_turns, cotangent,
):
    rows, elems = start_state.shape
    basis = rows // VARS
    devices = lax.axis_size("dom")
    fb = up_to(face_trace.shape[1], 8)
    pitch = up_to(basis, 16)
    frows = up_to(VARS * fb + 8, 16)
    full, faces, slots = (rows, elems), (VARS * fb, 4 * elems), (SLOTS, up_to(frows, 128))
    args = (
        start_state, cotangent, material, geometry, clusters.reshape(1, elems), neighbours,
        orientation, stiffness, face_trace.transpose(1, 0, 2), face_lift.transpose(2, 0, 1),
        face_turns,
    )
    scratch = [x.shape for x in args[:4]] + [x.shape for x in args[7:]]
    scratch += [full] * 10
    scratch += [(STEPS * rows, elems)] + [(STEPS * rows, FINE_DEV)] * 2
    scratch += [faces] * 8 + [slots] * 8
    scratch += [(8 * TERMS, elems), (32, elems), (8 * STEPS, FINE_DEV), (8, FINE_DEV)]
    scratch += [(8, 4 * elems), (16, SLOTS)]
    scratch += [(3, pitch, pitch), (4, fb, pitch), (4, fb, pitch), (3, fb, fb)]
    packed = [(4 * pitch, 3 * pitch)] * 2 + [(4 * fb, 3 * pitch)] * 2
    packed += [(basis, 12 * fb)] * 2 + [(6 * fb, 6 * fb)] * 2
    packed += [(4 * elems, 4 * elems)] + [(SLOTS, 4 * elems)] * 2 + [(2 * FINE_DEV, elems)]
    packed += [(2 * frows, 4 * elems)] * 3
    args = [pltpu.with_memory_space_constraint(x, pltpu.HBM) for x in args]
    outs = pl.pallas_call(
        functools.partial(step_kernel, devices),
        out_shape=[
            jax.ShapeDtypeStruct((rows, elems), f32),
            jax.ShapeDtypeStruct((3, elems), f32),
        ],
        in_specs=[pl.BlockSpec(memory_space=pltpu.HBM)] * len(args),
        out_specs=[pl.BlockSpec(memory_space=pltpu.VMEM)] * 2,
        scratch_shapes=[pltpu.VMEM(s, f32) for s in scratch]
        + [pltpu.VMEM(s, bf16) for s in packed]
        + [pltpu.VMEM((1, elems), i32)]
        + [pltpu.VMEM((4, elems), i32)] * 3
        + [pltpu.SemaphoreType.DMA((len(args),))]
        + [pltpu.SemaphoreType.DMA((4 * LANES,))] * 2,
        compiler_params=pltpu.CompilerParams(
            vmem_limit_bytes=48 * 1024 * 1024, collective_id=0, has_side_effects=True
        ),
        name="ader_step",
    )(*args)
    return pl.pallas_call(
        finish_kernel,
        out_shape=[jax.ShapeDtypeStruct(x.shape, f32) for x in outs],
        in_specs=[pl.BlockSpec(memory_space=pltpu.VMEM)] * 2,
        out_specs=[pl.BlockSpec(memory_space=pl.ANY)] * 2,
        scratch_shapes=[pltpu.SemaphoreType.DMA((2,))],
        compiler_params=pltpu.CompilerParams(vmem_limit_bytes=2 * 1024 * 1024),
        name="finish",
    )(*outs)


def solution(mesh):
    return jax.shard_map(
        body,
        mesh=mesh,
        in_specs=(
            P(None, "dom"),
            P(None, "dom"),
            P(None, "dom"),
            P("dom"),
            P(None, "dom"),
            P(None, "dom"),
            P(),
            P(),
            P(),
            P(),
            P(None, "dom"),
        ),
        out_specs=(P(None, "dom"), P(None, "dom")),
        check_vma=False,
    )
```

profile of v0, /device:TPU:0, one launch (start us, length us, event | category | flops | bytes accessed | tf_op | source)
XLA Modules:
  0.0 33.8 jit_solution(9498298304631749040)
XLA Ops:
  0.6 32.2 %ader_step.1 = (f32[504,256]{1,0:T(8,128)S(1)}, f32[3,256]{1,0:T(4,128)S(1)}) custom-call(f32[504,256]{1,0:T(8,128)} %state_in.1, f32[504,256]{1,0:T(8,128)} %cot_in.1, f32[3,256]{1,0:T(4,128)} %mat_in.1, f32[3,256]{1,0:T(4,128)} %geo_in.1, s32[1,256]{1,0:T(1,128)} %bitcast.5, s32[4,256]{1,0:T(4,128)} %neighbours_in.1, s32[4,256]{1,0:T(4,128)} %orientation_in.1, ...), custom_call_target="tpu_custom_call" | custom-call | tf_op jit(solution)/shard_map/ader_step/pallas_call | solution.py:771
  32.9 0.8 %finish.1 = (f32[504,256]{1,0:T(8,128)}, f32[3,256]{1,0:T(4,128)}) custom-call(f32[504,256]{1,0:T(8,128)S(1)} %get-tuple-element.4.final, f32[3,256]{1,0:T(4,128)S(1)} %get-tuple-element.5.grad), custom_call_target="tpu_custom_call" | custom-call | tf_op jit(solution)/shard_map/finish/pallas_call | solution.py:790
where the time goes:
time: 34 us; the launch traced here: 33.8 us
  Pallas kernels  33 us (97%)
  between operations  0.8 us (2%)
    pallas_call x1, Pallas kernels, body(): pl.pallas_call(functools.partial(step_kernel, devices), out_shape=[jax.Sh...  32.2 us
    pallas_call x1, Pallas kernels, body(): pl.pallas_call(finish_kernel, out_shape=[jax.ShapeDtypeStruct(x.shape, f3...  0.81 us

commit v1 on v0

--- a/solution.py
+++ b/solution.py
@@ -225,8 +225,8 @@
 def local_outer(own_hl, hot, turn, tn, out, fb, elems, f):
     rows = own_hl.shape[0] // 2
     cols = slice(f * elems, (f + 1) * elems)
-    y = mm(own_hl[...], hot[:, cols])
-    raw = y[: VARS * fb] + y[rows : rows + VARS * fb]
+    high, low = [mm(own_hl[n * rows : (n + 1) * rows, :], hot[:, cols]) for n in range(2)]
+    raw = high[: VARS * fb] + low[: VARS * fb]
     turned = turn_blocks(tn, split_rows(raw, fb), turn[f : f + 1, :])
     out[:, cols] = jnp.concatenate(turned, axis=0)
 
@@ -567,6 +567,12 @@
     seed2 = blocks(cot, size)
     faces_cot(seed2, lt, tnt, turn, extra, fcon, con, lifted2, own_cot2, x_hl2, fb, elems)
     serve(hot_slot, x_hl2, tx0)
+
+    def scatter(own_cot, x_hl):
+        return [part(scatter_local, own_cot, x_hl, hot, fb, elems, g) for g in range(4)]
+
+    for piece in hot_fills + scatter(own_cot2, x_hl2):
+        piece()
     pl.semaphore_wait(barrier, LANES)
     sent0 = send_all(up, tx0, rx0, send_sems, recv_sems, 0)
 
@@ -581,15 +587,16 @@
         old = blocks(state, size) if k == 0 else blocks(q1, size, (k - 1) * count)
         put(q1, apply_step(ks, old, Mat(con, 8 * (k + 1), geo_ref)), k * count)
 
-    def scatter(own_cot, x_hl):
-        return [part(scatter_local, own_cot, x_hl, hot, fb, elems, g) for g in range(4)]
-
     def gather():
         return [
             part(local_outer, own_hl, hot, turn, tn, out_loc, fb, elems, f) for f in range(4)
         ]
 
-    weave([part(step1, k) for k in range(STEPS)], hot_fills + scatter(own_cot2, x_hl2))
+    def volume(out, window):
+        put(out, apply_step(kt, blocks(window, size), base))
+
+    for k in range(STEPS):
+        step1(k)
     for v in range(VARS):
         rows = slice(v * size, (v + 1) * size)
         terms = [A0 * state[rows, :]]
@@ -598,6 +605,9 @@
         later = add(*[c * t if c != 1.0 else t for c, t in zip(C_OVER_A, terms)])
         wc[rows, :] = jnp.where(is_fine, 0.0, later)
     trace_faces(tr, w1, own, own_hl, fb, elems)
+    for piece in gather():
+        piece()
+    volume(vol1, w1)
     put(direct2, apply_back(ks, seed2, base))
     for copy in sent0:
         copy.wait()
@@ -634,15 +644,16 @@
         else:
             seed1[...] = widen(jnp.concatenate(r, axis=0), hot_c[...], wide) + cot[...]
 
-    def volume(out, window):
-        put(out, apply_step(kt, blocks(window, size), base))
-
-    weave([part(back2, k) for k in range(STEPS - 1, -1, -1)], gather() + [part(volume, vol1, w1)])
+    for k in range(STEPS - 1, -1, -1):
+        back2(k)
     faces_cot(
         blocks(seed1, size), lt, tnt, turn, None, fcon, con, lifted1, own_cot1, x_hl1, fb, elems
     )
     serve(hot_slot, x_hl1, tx3)
     sent3 = send_all(up, tx3, rx3, send_sems, recv_sems, 2 * LANES)
+    for piece in scatter(own_cot1, x_hl1):
+        piece()
+    put(cur, apply_back(ks, blocks(seed1, size), base))
     for copy in sent1:
         copy.wait()
 
@@ -658,12 +669,8 @@
         old = start if k == 0 else blocks(q2, size, (k - 1) * count)
         put(q2, apply_step(ks, old, Mat(con_f, 8 * k, geo_f)), k * count)
 
-    def direct1():
-        put(cur, apply_back(ks, blocks(seed1, size), base))
-
-    weave(
-        [part(step2, k) for k in range(STEPS)], scatter(own_cot1, x_hl1) + [direct1]
-    )
+    for k in range(STEPS):
+        step2(k)
     window = [
         add(first[v], *[
             q2[k * count + v * size : k * count + (v + 1) * size, :] for k in range(STEPS)
@@ -671,11 +678,11 @@
         for v in range(VARS)
     ]
     w2[...] = widen(jnp.concatenate(window, axis=0), hot_c[...], wide) + wc[...]
-    sums, speed = face_sums(lifted1, jump, flux, half_speed, fb, elems)
     trace_faces(tr, w2, own, own_hl, fb, elems)
     serve(hot_in, own_hl, tx2)
     sent2 = send_all(down, tx2, rx2, send_sems, recv_sems, 3 * LANES)
 
+    sums, speed = face_sums(lifted1, jump, flux, half_speed, fb, elems)
     sums = plus(sums, group_sums(blocks(seed1, size), blocks(vol1, size)))
     fine_sums = None
     for k in range(STEPS):

time: 34 us -> 32.6 us (0.959)
  Pallas kernels: 33 us -> 31.6 us
    pallas_call x1, Pallas kernels: 32.2 us -> 30.8 us  [body(): pl.pallas_call(functools.partial(step_kernel, devices), out_shape=[jax.Sh...]
where the time goes in v1:
time: 32.6 us; the launch traced here: 32.4 us
  Pallas kernels  31.6 us (97%)
  between operations  0.8 us (2%)
    pallas_call x1, Pallas kernels, body(): pl.pallas_call(functools.partial(step_kernel, devices), out_shape=[jax.Sh...  30.8 us
    pallas_call x1, Pallas kernels, body(): pl.pallas_call(finish_kernel, out_shape=[jax.ShapeDtypeStruct(x.shape, f3...  0.81 us

profile of v1, /device:TPU:0, one launch (start us, length us, event | category | flops | bytes accessed | tf_op | source)
XLA Modules:
  0.0 32.4 jit_solution(14757851409803545101)
XLA Ops:
  0.6 30.8 %ader_step.1 = (f32[504,256]{1,0:T(8,128)S(1)}, f32[3,256]{1,0:T(4,128)S(1)}) custom-call(f32[504,256]{1,0:T(8,128)} %state_in.1, f32[504,256]{1,0:T(8,128)} %cot_in.1, f32[3,256]{1,0:T(4,128)} %mat_in.1, f32[3,256]{1,0:T(4,128)} %geo_in.1, s32[1,256]{1,0:T(1,128)} %bitcast.5, s32[4,256]{1,0:T(4,128)} %neighbours_in.1, s32[4,256]{1,0:T(4,128)} %orientation_in.1, ...), custom_call_target="tpu_custom_call" | custom-call | tf_op jit(solution)/shard_map/ader_step/pallas_call | solution.py:778
  31.4 0.8 %finish.1 = (f32[504,256]{1,0:T(8,128)}, f32[3,256]{1,0:T(4,128)}) custom-call(f32[504,256]{1,0:T(8,128)S(1)} %get-tuple-element.4.final, f32[3,256]{1,0:T(4,128)S(1)} %get-tuple-element.5.grad), custom_call_target="tpu_custom_call" | custom-call | tf_op jit(solution)/shard_map/finish/pallas_call | solution.py:797

commit v2 on v1

--- a/solution.py
+++ b/solution.py
@@ -57,6 +57,19 @@
 def left3(a):
     high = a.astype(bf16).astype(f32)
     return jnp.concatenate([high, a - high, high], axis=1).astype(bf16)
+
+
+def left2(a):
+    high = a.astype(bf16).astype(f32)
+    upper = jnp.concatenate([high, high], axis=1)
+    lower = jnp.concatenate([a - high, jnp.zeros(a.shape, f32)], axis=1)
+    return jnp.concatenate([upper, lower], axis=0).astype(bf16)
+
+
+def apply2(mat, x):
+    y = mm(mat[...], stack2(x, x.shape[0]))
+    half = y.shape[0] // 2
+    return y[:half] + y[half:]
 
 
 def stack2(x, rows):
@@ -138,7 +151,7 @@
 
 def products(mat, values):
     size, width = values[0].shape
-    pitch = mat.shape[0] // 4
+    pitch = mat.shape[2] // 3
     out = {}
     if width == FINE_DEV:
         groups = PAIRS
@@ -147,11 +160,11 @@
     for names, start, count in groups:
         x = [values[v] for v in names]
         x = x[0] if len(x) == 1 else jnp.concatenate(x, axis=1)
-        y = mm(mat[start * pitch : (start + count) * pitch, :], right3(x, pitch))
+        y = mm(mat[start, : count * size, :], right3(x, pitch))
         for n, v in enumerate(names):
             for i in range(count):
                 out[v, (start + i) % 3] = y[
-                    i * pitch : i * pitch + size, n * width : (n + 1) * width
+                    i * size : (i + 1) * size, n * width : (n + 1) * width
                 ]
     return lambda v, axis: out[v, axis]
 
@@ -207,28 +220,34 @@
 
 def turn_blocks(mat, x, which):
     fb = x[0].shape[0]
-    first, second = which == 0, which == 1
-    out = []
+    pick = [(w == 0, w == 1) for w in which]
+    out = [None] * len(x)
+    order = [f * VARS + v for f in range(len(which)) for v in range(VARS - 1)]
+    order += [f * VARS + VARS - 1 for f in range(len(which))]
     for n in range(0, len(x), 2):
-        pair = x[n] if n + 1 == len(x) else jnp.concatenate(x[n : n + 2], axis=0)
-        y = mm(mat[...], right3(pair, 2 * fb))
-        for i in range(min(2, len(x) - n)):
+        names = order[n : n + 2]
+        pair = [x[b] for b in names]
+        y = mm(mat[...], right3(jnp.concatenate(pair, axis=0), 2 * fb))
+        for i, b in enumerate(names):
+            first, second = pick[b // VARS]
             part = [y[o * 2 * fb + i * fb : o * 2 * fb + (i + 1) * fb] for o in range(3)]
-            out.append(jnp.where(first, part[0], jnp.where(second, part[1], part[2])))
-    return out
+            out[b] = jnp.where(first, part[0], jnp.where(second, part[1], part[2]))
+    return [out[n : n + VARS] for n in range(0, len(x), VARS)]
 
 
 def split_rows(x, fb):
     return [x[v * fb : (v + 1) * fb] for v in range(VARS)]
 
 
-def local_outer(own_hl, hot, turn, tn, out, fb, elems, f):
+def local_outer(own_hl, hot, turn, tn, out, fb, elems, faces):
     rows = own_hl.shape[0] // 2
-    cols = slice(f * elems, (f + 1) * elems)
-    high, low = [mm(own_hl[n * rows : (n + 1) * rows, :], hot[:, cols]) for n in range(2)]
-    raw = high[: VARS * fb] + low[: VARS * fb]
-    turned = turn_blocks(tn, split_rows(raw, fb), turn[f : f + 1, :])
-    out[:, cols] = jnp.concatenate(turned, axis=0)
+    raw = []
+    for f in faces:
+        y = mm(own_hl[...], hot[:, f * elems : (f + 1) * elems])
+        raw += split_rows(y[: VARS * fb] + y[rows : rows + VARS * fb], fb)
+    turned = turn_blocks(tn, raw, [turn[f : f + 1, :] for f in faces])
+    for f, x in zip(faces, turned):
+        out[:, f * elems : (f + 1) * elems] = jnp.concatenate(x, axis=0)
 
 
 def serve(hot_in, own_hl, tx):
@@ -281,7 +300,7 @@
 
 def far_side(rx, slot_turn, tn, hot_slot, out_loc, fb):
     rows = up_to(VARS * fb, 16)
-    turned = turn_blocks(tn, split_rows(flipped(rx), fb), slot_turn[0:1, :])
+    turned = turn_blocks(tn, split_rows(flipped(rx), fb), [slot_turn[0:1, :]])[0]
     high_low = stack2(jnp.concatenate(turned, axis=0), rows)
 
     def far(f, elems):
@@ -305,7 +324,7 @@
             jump_ref[v * fb : (v + 1) * fb, cols] = jump
             flux_ref[v * fb : (v + 1) * fb, cols] = flux
             fluxes[v].append(flux)
-    return [mm(lf[...], right3(jnp.concatenate(x, axis=0), 4 * fb)) for x in fluxes]
+    return [apply2(lf, jnp.concatenate(x, axis=0)) for x in fluxes]
 
 
 def face_sums(lifted, jump_ref, flux_ref, half_speed, fb, elems):
@@ -327,25 +346,24 @@
         y = mm(lt[...], right3(seed[v], lt.shape[1] // 3))
         for f in range(4):
             lifted[v * fb : (v + 1) * fb, f * elems : (f + 1) * elems] = y[f * fb : (f + 1) * fb]
-    for f in range(4):
-        cols = slice(f * elems, (f + 1) * elems)
-        r = split_rows(lifted[:, cols], fb)
-        back = face_rows_back(f, r, face_consts(f, fcon, con))
+    for faces in ((0, 1), (2, 3)):
         x = []
-        for v in range(VARS):
-            side = half_speed * r[v]
-            own_cot[v * fb : (v + 1) * fb, cols] = add(side, back[v])
-            x.append(-side if back[v] is None else back[v] - side)
-        turned = turn_blocks(tnt, x, turn[f : f + 1, :])
-        if extra is not None:
-            turned.append(extra[:, cols])
-        high, low = halves(padded(jnp.concatenate(turned, axis=0), rows))
-        x_hl[:rows, cols] = high
-        x_hl[rows:, cols] = low
-
-
-def send_cot(hot_slot, x_hl, tx):
-    serve(hot_slot, x_hl, tx)
+        for f in faces:
+            cols = slice(f * elems, (f + 1) * elems)
+            r = split_rows(lifted[:, cols], fb)
+            back = face_rows_back(f, r, face_consts(f, fcon, con))
+            for v in range(VARS):
+                side = half_speed * r[v]
+                own_cot[v * fb : (v + 1) * fb, cols] = add(side, back[v])
+                x.append(-side if back[v] is None else back[v] - side)
+        turned = turn_blocks(tnt, x, [turn[f : f + 1, :] for f in faces])
+        for f, y in zip(faces, turned):
+            cols = slice(f * elems, (f + 1) * elems)
+            if extra is not None:
+                y.append(extra[:, cols])
+            high, low = halves(padded(jnp.concatenate(y, axis=0), rows))
+            x_hl[:rows, cols] = high
+            x_hl[rows:, cols] = low
 
 
 def scatter_local(own_cot, x_hl, hot, fb, elems, g):
@@ -365,7 +383,7 @@
     out = []
     for v in range(VARS):
         x = [own_cot[v * fb : (v + 1) * fb, g * elems : (g + 1) * elems] for g in range(4)]
-        out.append(mm(trt[...], right3(jnp.concatenate(x, axis=0), 4 * fb)))
+        out.append(apply2(trt, jnp.concatenate(x, axis=0)))
     return out
 
 
@@ -551,10 +569,10 @@
     constants(mat_ref, geo_ref, con, fcon)
     trace = jnp.concatenate(pitched(t_pad, [face_trace[:, g, :] for g in range(4)]), axis=0)
     tr[...] = left3(trace)
-    trt[...] = left3(trace.T)[:size]
+    trt[...] = left2(trace.T[:size])
     lift = jnp.concatenate(pitched(l_pad, [-face_lift[:, f, :] for f in range(4)]), axis=0)
     lt[...] = left3(lift)
-    lf[...] = left3(lift.T)[:size]
+    lf[...] = left2(lift.T[:size])
     turns = [face_turns[o] for o in range(3)]
     tn[...] = turn_matrix(n_pad, turns)
     tnt[...] = turn_matrix(n_pad, [x.T for x in turns])
@@ -577,9 +595,10 @@
     sent0 = send_all(up, tx0, rx0, send_sems, recv_sems, 0)
 
     stiff = pitched(k_pad, [stiffness[d] for d in range(3)])
-    ks[...] = left3(jnp.concatenate(stiff + stiff[:1], axis=0))
-    stiff = [x.T for x in stiff]
-    kt[...] = left3(jnp.concatenate(stiff + stiff[:1], axis=0))
+    for mat, axes in ((ks, stiff), (kt, [x.T for x in stiff])):
+        for n in range(3):
+            order = [axes[(n + i) % 3][:size] for i in range(3)]
+            mat[n] = left3(jnp.concatenate(order, axis=0))
     is_fine = fine[...] == 1
     loads[10].wait()
 
@@ -589,7 +608,8 @@
 
     def gather():
         return [
-            part(local_outer, own_hl, hot, turn, tn, out_loc, fb, elems, f) for f in range(4)
+            part(local_outer, own_hl, hot, turn, tn, out_loc, fb, elems, faces)
+            for faces in ((0, 1), (2, 3))
         ]
 
     def volume(out, window):
@@ -607,7 +627,6 @@
     trace_faces(tr, w1, own, own_hl, fb, elems)
     for piece in gather():
         piece()
-    volume(vol1, w1)
     put(direct2, apply_back(ks, seed2, base))
     for copy in sent0:
         copy.wait()
@@ -654,6 +673,7 @@
     for piece in scatter(own_cot1, x_hl1):
         piece()
     put(cur, apply_back(ks, blocks(seed1, size), base))
+    volume(vol1, w1)
     for copy in sent1:
         copy.wait()
 
@@ -770,8 +790,8 @@
     scratch += [(8 * TERMS, elems), (32, elems), (8 * STEPS, FINE_DEV), (8, FINE_DEV)]
     scratch += [(8, 4 * elems), (16, SLOTS)]
     scratch += [(3, pitch, pitch), (4, fb, pitch), (4, fb, pitch), (3, fb, fb)]
-    packed = [(4 * pitch, 3 * pitch)] * 2 + [(4 * fb, 3 * pitch)] * 2
-    packed += [(basis, 12 * fb)] * 2 + [(6 * fb, 6 * fb)] * 2
+    packed = [(3, 3 * basis, 3 * pitch)] * 2 + [(4 * fb, 3 * pitch)] * 2
+    packed += [(2 * basis, 8 * fb)] * 2 + [(6 * fb, 6 * fb)] * 2
     packed += [(4 * elems, 4 * elems)] + [(SLOTS, 4 * elems)] * 2 + [(2 * FINE_DEV, elems)]
     packed += [(2 * frows, 4 * elems)] * 3
     args = [pltpu.with_memory_space_constraint(x, pltpu.HBM) for x in args]

time: 32.6 us -> 32 us (0.982)
  Pallas kernels: 31.6 us -> 31 us
    pallas_call x1, Pallas kernels: 30.8 us -> 30.2 us  [body(): pl.pallas_call(functools.partial(step_kernel, devices), out_shape=[jax.Sh...]
where the time goes in v2:
time: 32 us; the launch traced here: 31.8 us
  Pallas kernels  31 us (97%)
  between operations  0.8 us (2%)
    pallas_call x1, Pallas kernels, body(): pl.pallas_call(functools.partial(step_kernel, devices), out_shape=[jax.Sh...  30.2 us
    pallas_call x1, Pallas kernels, body(): pl.pallas_call(finish_kernel, out_shape=[jax.ShapeDtypeStruct(x.shape, f3...  0.81 us

profile of v2, /device:TPU:0, one launch (start us, length us, event | category | flops | bytes accessed | tf_op | source)
XLA Modules:
  0.0 31.8 jit_solution(6273200538579005165)
XLA Ops:
  0.6 30.2 %ader_step.1 = (f32[504,256]{1,0:T(8,128)S(1)}, f32[3,256]{1,0:T(4,128)S(1)}) custom-call(f32[504,256]{1,0:T(8,128)} %state_in.1, f32[504,256]{1,0:T(8,128)} %cot_in.1, f32[3,256]{1,0:T(4,128)} %mat_in.1, f32[3,256]{1,0:T(4,128)} %geo_in.1, s32[1,256]{1,0:T(1,128)} %bitcast.5, s32[4,256]{1,0:T(4,128)} %neighbours_in.1, s32[4,256]{1,0:T(4,128)} %orientation_in.1, ...), custom_call_target="tpu_custom_call" | custom-call | tf_op jit(solution)/shard_map/ader_step/pallas_call | solution.py:798
  30.9 0.8 %finish.1 = (f32[504,256]{1,0:T(8,128)}, f32[3,256]{1,0:T(4,128)}) custom-call(f32[504,256]{1,0:T(8,128)S(1)} %get-tuple-element.4.final, f32[3,256]{1,0:T(4,128)S(1)} %get-tuple-element.5.grad), custom_call_target="tpu_custom_call" | custom-call | tf_op jit(solution)/shard_map/finish/pallas_call | solution.py:817

commit v3 on v2

--- a/solution.py
+++ b/solution.py
@@ -589,8 +589,6 @@
     def scatter(own_cot, x_hl):
         return [part(scatter_local, own_cot, x_hl, hot, fb, elems, g) for g in range(4)]
 
-    for piece in hot_fills + scatter(own_cot2, x_hl2):
-        piece()
     pl.semaphore_wait(barrier, LANES)
     sent0 = send_all(up, tx0, rx0, send_sems, recv_sems, 0)
 
@@ -615,6 +613,8 @@
     def volume(out, window):
         put(out, apply_step(kt, blocks(window, size), base))
 
+    for piece in hot_fills + scatter(own_cot2, x_hl2):
+        piece()
     for k in range(STEPS):
         step1(k)
     for v in range(VARS):
@@ -627,7 +627,6 @@
     trace_faces(tr, w1, own, own_hl, fb, elems)
     for piece in gather():
         piece()
-    put(direct2, apply_back(ks, seed2, base))
     for copy in sent0:
         copy.wait()
 
@@ -638,6 +637,7 @@
     serve(hot_in, own_hl, tx1)
     sent1 = send_all(down, tx1, rx1, send_sems, recv_sems, LANES)
 
+    put(direct2, apply_back(ks, seed2, base))
     back = faces_back(own_cot2, rx0, hot_in, trt, fb, elems)
     back = [a + b for a, b in zip(back, blocks(direct2, size))]
     put(coarse, [jnp.where(is_fine, 0.0, x) for x in back])
@@ -670,8 +670,6 @@
     )
     serve(hot_slot, x_hl1, tx3)
     sent3 = send_all(up, tx3, rx3, send_sems, recv_sems, 2 * LANES)
-    for piece in scatter(own_cot1, x_hl1):
-        piece()
     put(cur, apply_back(ks, blocks(seed1, size), base))
     volume(vol1, w1)
     for copy in sent1:
@@ -704,6 +702,8 @@
 
     sums, speed = face_sums(lifted1, jump, flux, half_speed, fb, elems)
     sums = plus(sums, group_sums(blocks(seed1, size), blocks(vol1, size)))
+    for piece in scatter(own_cot1, x_hl1):
+        piece()
     fine_sums = None
     for k in range(STEPS):
         fine_sums = plus(

time: 32 us -> 31.9 us (level)
  no operation moved by 1% of the time
where the time goes in v3:
time: 31.9 us; the launch traced here: 31.7 us
  Pallas kernels  30.9 us (97%)
  between operations  0.8 us (3%)
    pallas_call x1, Pallas kernels, body(): pl.pallas_call(functools.partial(step_kernel, devices), out_shape=[jax.Sh...  30.1 us
    pallas_call x1, Pallas kernels, body(): pl.pallas_call(finish_kernel, out_shape=[jax.ShapeDtypeStruct(x.shape, f3...  0.81 us

profile of v3, /device:TPU:0, one launch (start us, length us, event | category | flops | bytes accessed | tf_op | source)
XLA Modules:
  0.0 31.7 jit_solution(5254193610121247548)
XLA Ops:
  0.6 30.1 %ader_step.1 = (f32[504,256]{1,0:T(8,128)S(1)}, f32[3,256]{1,0:T(4,128)S(1)}) custom-call(f32[504,256]{1,0:T(8,128)} %state_in.1, f32[504,256]{1,0:T(8,128)} %cot_in.1, f32[3,256]{1,0:T(4,128)} %mat_in.1, f32[3,256]{1,0:T(4,128)} %geo_in.1, s32[1,256]{1,0:T(1,128)} %bitcast.5, s32[4,256]{1,0:T(4,128)} %neighbours_in.1, s32[4,256]{1,0:T(4,128)} %orientation_in.1, ...), custom_call_target="tpu_custom_call" | custom-call | tf_op jit(solution)/shard_map/ader_step/pallas_call | solution.py:798
  30.7 0.8 %finish.1 = (f32[504,256]{1,0:T(8,128)}, f32[3,256]{1,0:T(4,128)}) custom-call(f32[504,256]{1,0:T(8,128)S(1)} %get-tuple-element.4.final, f32[3,256]{1,0:T(4,128)S(1)} %get-tuple-element.5.grad), custom_call_target="tpu_custom_call" | custom-call | tf_op jit(solution)/shard_map/finish/pallas_call | solution.py:817

commit v4 on v3

--- a/solution.py
+++ b/solution.py
@@ -585,6 +585,8 @@
     seed2 = blocks(cot, size)
     faces_cot(seed2, lt, tnt, turn, extra, fcon, con, lifted2, own_cot2, x_hl2, fb, elems)
     serve(hot_slot, x_hl2, tx0)
+    for piece in hot_fills:
+        piece()
 
     def scatter(own_cot, x_hl):
         return [part(scatter_local, own_cot, x_hl, hot, fb, elems, g) for g in range(4)]
@@ -613,7 +615,7 @@
     def volume(out, window):
         put(out, apply_step(kt, blocks(window, size), base))
 
-    for piece in hot_fills + scatter(own_cot2, x_hl2):
+    for piece in scatter(own_cot2, x_hl2):
         piece()
     for k in range(STEPS):
         step1(k)
@@ -670,6 +672,8 @@
     )
     serve(hot_slot, x_hl1, tx3)
     sent3 = send_all(up, tx3, rx3, send_sems, recv_sems, 2 * LANES)
+    for piece in scatter(own_cot1, x_hl1):
+        piece()
     put(cur, apply_back(ks, blocks(seed1, size), base))
     volume(vol1, w1)
     for copy in sent1:
@@ -702,8 +706,6 @@
 
     sums, speed = face_sums(lifted1, jump, flux, half_speed, fb, elems)
     sums = plus(sums, group_sums(blocks(seed1, size), blocks(vol1, size)))
-    for piece in scatter(own_cot1, x_hl1):
-        piece()
     fine_sums = None
     for k in range(STEPS):
         fine_sums = plus(

time: 31.9 us -> 31.2 us (0.978)
  Pallas kernels: 30.9 us -> 30.2 us
    pallas_call x1, Pallas kernels: 30.1 us -> 29.4 us  [body(): pl.pallas_call(functools.partial(step_kernel, devices), out_shape=[jax.Sh...]
where the time goes in v4:
time: 31.2 us; the launch traced here: 31 us
  Pallas kernels  30.2 us (97%)
  between operations  0.8 us (3%)
    pallas_call x1, Pallas kernels, body(): pl.pallas_call(functools.partial(step_kernel, devices), out_shape=[jax.Sh...  29.4 us
    pallas_call x1, Pallas kernels, body(): pl.pallas_call(finish_kernel, out_shape=[jax.ShapeDtypeStruct(x.shape, f3...  0.81 us

profile of v4, /device:TPU:0, one launch (start us, length us, event | category | flops | bytes accessed | tf_op | source)
XLA Modules:
  0.0 31.0 jit_solution(4212063404956696041)
XLA Ops:
  0.6 29.4 %ader_step.1 = (f32[504,256]{1,0:T(8,128)S(1)}, f32[3,256]{1,0:T(4,128)S(1)}) custom-call(f32[504,256]{1,0:T(8,128)} %state_in.1, f32[504,256]{1,0:T(8,128)} %cot_in.1, f32[3,256]{1,0:T(4,128)} %mat_in.1, f32[3,256]{1,0:T(4,128)} %geo_in.1, s32[1,256]{1,0:T(1,128)} %bitcast.5, s32[4,256]{1,0:T(4,128)} %neighbours_in.1, s32[4,256]{1,0:T(4,128)} %orientation_in.1, ...), custom_call_target="tpu_custom_call" | custom-call | tf_op jit(solution)/shard_map/ader_step/pallas_call | solution.py:800
  30.1 0.8 %finish.1 = (f32[504,256]{1,0:T(8,128)}, f32[3,256]{1,0:T(4,128)}) custom-call(f32[504,256]{1,0:T(8,128)S(1)} %get-tuple-element.4.final, f32[3,256]{1,0:T(4,128)S(1)} %get-tuple-element.5.grad), custom_call_target="tpu_custom_call" | custom-call | tf_op jit(solution)/shard_map/finish/pallas_call | solution.py:819

commit v5 on v4

--- a/solution.py
+++ b/solution.py
@@ -405,9 +405,10 @@
     ]
 
 
-def send_all(peers, src, dst, send_sems, recv_sems, base=0):
+def send_all(peers, src, dst, send_sems, recv_sems, base, near):
+    last = [n for n in range(LANES - 1) if n not in near]
     copies = []
-    for n in reversed(range(LANES)):
+    for n in list(near) + [LANES - 1] + last:
         rows = pl.ds(n * CAP, CAP)
         copy = pltpu.make_async_remote_copy(
             src_ref=src.at[rows],
@@ -592,7 +593,7 @@
         return [part(scatter_local, own_cot, x_hl, hot, fb, elems, g) for g in range(4)]
 
     pl.semaphore_wait(barrier, LANES)
-    sent0 = send_all(up, tx0, rx0, send_sems, recv_sems, 0)
+    sent0 = send_all(up, tx0, rx0, send_sems, recv_sems, 0, range(REACH))
 
     stiff = pitched(k_pad, [stiffness[d] for d in range(3)])
     for mat, axes in ((ks, stiff), (kt, [x.T for x in stiff])):
@@ -637,7 +638,7 @@
     at = lax.broadcasted_iota(i32, (SLOTS, 4 * elems), 1)
     hot_in[...] = one_hot(at == key.astype(i32))
     serve(hot_in, own_hl, tx1)
-    sent1 = send_all(down, tx1, rx1, send_sems, recv_sems, LANES)
+    sent1 = send_all(down, tx1, rx1, send_sems, recv_sems, LANES, range(REACH, 2 * REACH))
 
     put(direct2, apply_back(ks, seed2, base))
     back = faces_back(own_cot2, rx0, hot_in, trt, fb, elems)
@@ -671,7 +672,7 @@
         blocks(seed1, size), lt, tnt, turn, None, fcon, con, lifted1, own_cot1, x_hl1, fb, elems
     )
     serve(hot_slot, x_hl1, tx3)
-    sent3 = send_all(up, tx3, rx3, send_sems, recv_sems, 2 * LANES)
+    sent3 = send_all(up, tx3, rx3, send_sems, recv_sems, 2 * LANES, range(REACH))
     for piece in scatter(own_cot1, x_hl1):
         piece()
     put(cur, apply_back(ks, blocks(seed1, size), base))
@@ -702,7 +703,7 @@
     w2[...] = widen(jnp.concatenate(window, axis=0), hot_c[...], wide) + wc[...]
     trace_faces(tr, w2, own, own_hl, fb, elems)
     serve(hot_in, own_hl, tx2)
-    sent2 = send_all(down, tx2, rx2, send_sems, recv_sems, 3 * LANES)
+    sent2 = send_all(down, tx2, rx2, send_sems, recv_sems, 3 * LANES, range(REACH, 2 * REACH))
 
     sums, speed = face_sums(lifted1, jump, flux, half_speed, fb, elems)
     sums = plus(sums, group_sums(blocks(seed1, size), blocks(vol1, size)))

time: 31.2 us -> 30.4 us (0.974)
  Pallas kernels: 30.2 us -> 29.4 us
    pallas_call x1, Pallas kernels: 29.4 us -> 28.6 us  [body(): pl.pallas_call(functools.partial(step_kernel, devices), out_shape=[jax.Sh...]
where the time goes in v5:
time: 30.4 us; the launch traced here: 30.2 us
  Pallas kernels  29.4 us (97%)
  between operations  0.8 us (3%)
    pallas_call x1, Pallas kernels, body(): pl.pallas_call(functools.partial(step_kernel, devices), out_shape=[jax.Sh...  28.6 us
    pallas_call x1, Pallas kernels, body(): pl.pallas_call(finish_kernel, out_shape=[jax.ShapeDtypeStruct(x.shape, f3...  0.81 us

profile of v5, /device:TPU:0, one launch (start us, length us, event | category | flops | bytes accessed | tf_op | source)
XLA Modules:
  0.0 30.2 jit_solution(8933144520329992356)
XLA Ops:
  0.6 28.6 %ader_step.1 = (f32[504,256]{1,0:T(8,128)S(1)}, f32[3,256]{1,0:T(4,128)S(1)}) custom-call(f32[504,256]{1,0:T(8,128)} %state_in.1, f32[504,256]{1,0:T(8,128)} %cot_in.1, f32[3,256]{1,0:T(4,128)} %mat_in.1, f32[3,256]{1,0:T(4,128)} %geo_in.1, s32[1,256]{1,0:T(1,128)} %bitcast.5, s32[4,256]{1,0:T(4,128)} %neighbours_in.1, s32[4,256]{1,0:T(4,128)} %orientation_in.1, ...), custom_call_target="tpu_custom_call" | custom-call | tf_op jit(solution)/shard_map/ader_step/pallas_call | solution.py:801
  29.3 0.8 %finish.1 = (f32[504,256]{1,0:T(8,128)}, f32[3,256]{1,0:T(4,128)}) custom-call(f32[504,256]{1,0:T(8,128)S(1)} %get-tuple-element.4.final, f32[3,256]{1,0:T(4,128)S(1)} %get-tuple-element.5.grad), custom_call_target="tpu_custom_call" | custom-call | tf_op jit(solution)/shard_map/finish/pallas_call | solution.py:820

commit v6 on v5

--- a/solution.py
+++ b/solution.py
@@ -408,7 +408,7 @@
 def send_all(peers, src, dst, send_sems, recv_sems, base, near):
     last = [n for n in range(LANES - 1) if n not in near]
     copies = []
-    for n in list(near) + [LANES - 1] + last:
+    for n in list(reversed(near)) + [LANES - 1] + last:
         rows = pl.ds(n * CAP, CAP)
         copy = pltpu.make_async_remote_copy(
             src_ref=src.at[rows],

time: 30.4 us -> 30.8 us (1.013)
  Pallas kernels: 29.4 us -> 29.8 us
    pallas_call x1, Pallas kernels: 28.6 us -> 29 us  [body(): pl.pallas_call(functools.partial(step_kernel, devices), out_shape=[jax.Sh...]
where the time goes in v6:
time: 30.8 us; the launch traced here: 30.6 us
  Pallas kernels  29.8 us (97%)
  between operations  0.8 us (3%)
    pallas_call x1, Pallas kernels, body(): pl.pallas_call(functools.partial(step_kernel, devices), out_shape=[jax.Sh...  29 us
    pallas_call x1, Pallas kernels, body(): pl.pallas_call(finish_kernel, out_shape=[jax.ShapeDtypeStruct(x.shape, f3...  0.81 us

profile of v6, /device:TPU:0, one launch (start us, length us, event | category | flops | bytes accessed | tf_op | source)
XLA Modules:
  0.0 30.6 jit_solution(17309965867635213132)
XLA Ops:
  0.6 29.0 %ader_step.1 = (f32[504,256]{1,0:T(8,128)S(1)}, f32[3,256]{1,0:T(4,128)S(1)}) custom-call(f32[504,256]{1,0:T(8,128)} %state_in.1, f32[504,256]{1,0:T(8,128)} %cot_in.1, f32[3,256]{1,0:T(4,128)} %mat_in.1, f32[3,256]{1,0:T(4,128)} %geo_in.1, s32[1,256]{1,0:T(1,128)} %bitcast.5, s32[4,256]{1,0:T(4,128)} %neighbours_in.1, s32[4,256]{1,0:T(4,128)} %orientation_in.1, ...), custom_call_target="tpu_custom_call" | custom-call | tf_op jit(solution)/shard_map/ader_step/pallas_call | solution.py:801
  29.6 0.8 %finish.1 = (f32[504,256]{1,0:T(8,128)}, f32[3,256]{1,0:T(4,128)}) custom-call(f32[504,256]{1,0:T(8,128)S(1)} %get-tuple-element.4.final, f32[3,256]{1,0:T(4,128)S(1)} %get-tuple-element.5.grad), custom_call_target="tpu_custom_call" | custom-call | tf_op jit(solution)/shard_map/finish/pallas_call | solution.py:820
